TPU v7x, 32 devices: a whole 2x2x4 slice. The times are simulated.
32 devices in a mesh: node: 8 (over z, x), mp: 4 (over y, core).
Axes of the slice: x: 2, y: 2, z: 4, core: 2. Of those that a mesh axis runs over, the one named last changes fastest.
Arguments:
- queries: bfloat16 [32, 64, 128], P('node', 'mp'), may hold values from -8 to 8
- root_keys: bfloat16 [16384, 8, 128], P('node', 'mp'), may hold values from -6 to 6
- root_values: bfloat16 [16384, 8, 128], P('node', 'mp'), may hold values from -6 to 6
- mid_keys: bfloat16 [8, 1024, 8, 128], P('node', None, 'mp'), may hold values from -6 to 6
- mid_values: bfloat16 [8, 1024, 8, 128], P('node', None, 'mp'), may hold values from -6 to 6
- leaf_keys: bfloat16 [32, 256, 8, 128], P('node', None, 'mp'), may hold values from -6 to 6
- leaf_values: bfloat16 [32, 256, 8, 128], P('node', None, 'mp'), may hold values from -6 to 6
- mid_length: int32 [8], replicated, may hold values from 1 to 1024
- leaf_length: int32 [32], P('node'), may hold values from 1 to 256
- branch_mid: int32 [32, 1], replicated, may hold values from 0 to 7; in each aligned block of 32 rows (0 to 31, 32 to 63, ...) at most 8 rows name the same one
- residual: bfloat16 [32, 8192], P(None, 'node'), may hold values from -6 to 6
- norm_gain: float32 [8192], P('node'), may hold values from 0.5 to 1.5
- out_weight: bfloat16 [8192, 8192], P('mp', 'node'), may hold values from -0.0625 to 0.0625
- gate_weight: bfloat16 [8192, 28672], P('node', 'mp'), may hold values from -0.0625 to 0.0625
- up_weight: bfloat16 [8192, 28672], P('node', 'mp'), may hold values from -0.0625 to 0.0625
- down_weight: bfloat16 [28672, 8192], P('mp', 'node'), may hold values from -0.03125 to 0.03125
Outputs:
- layer_out: bfloat16 [32, 8192], P('mp', 'node')
Inputs may be any that keep to these rules, and one draw needn't show every extreme that they name: `branch_mid`: every inner tree node lies on the path of 1 to 8 branches, and some node on exactly 8.
All inputs are finite; a program needn't handle non-finite values.
Results may differ from a plain program's by a relative error of at most 0.015.
Values may be sent and summed in bfloat16 or wider, within the bound.
A program may use at most 128 MiB of HBM per device.

v0:
```python
import jax
import jax.numpy as jnp
from jax import lax
from jax.sharding import PartitionSpec as P

D = 8192
CAP = 8
masked_score = -1e30
norm_eps = 1e-05


def partial_scores(grouped, key_block, value_block, usable, scaling):
    scores = (
        jnp.einsum("bkgd,lkd->bkgl", grouped, key_block, preferred_element_type=jnp.float32)
        * scaling
    )
    masking = usable[:, None, None, :]
    scores = jnp.where(masking, scores, masked_score)
    highest = jnp.max(scores, axis=-1)
    weights = jnp.where(masking, jnp.exp(scores - highest[..., None]), 0.0)
    weighted = jnp.einsum(
        "bkgl,lkd->bkgd",
        weights.astype(jnp.bfloat16),
        value_block,
        preferred_element_type=jnp.float32,
    )
    return (highest, jnp.sum(weights, axis=-1), weighted)


def combine_parts(earlier, later):
    highest = jnp.maximum(earlier[0], later[0])
    first_factor = jnp.exp(earlier[0] - highest)
    second_factor = jnp.exp(later[0] - highest)
    totals = earlier[1] * first_factor + later[1] * second_factor
    weighted = earlier[2] * first_factor[..., None] + later[2] * second_factor[..., None]
    return (highest, totals, weighted)


def on_device(
    queries,
    root_keys,
    root_values,
    mid_keys,
    mid_values,
    leaf_keys,
    leaf_values,
    mid_length,
    leaf_length,
    branch_mid,
    residual,
    norm_gain,
    out_weight,
    gate_weight,
    up_weight,
    down_weight,
):
    owned = queries.shape[0]
    local_heads = queries.shape[1]
    head_size = queries.shape[2]
    local_groups = root_keys.shape[1]
    group_size = local_heads // local_groups
    scaling = head_size ** (-0.5)
    node_count = lax.axis_size("node")
    gathered = lax.all_gather(queries, "node", axis=0, tiled=True)
    every_branch = gathered.shape[0]
    grouped = gathered.reshape(every_branch, local_groups, group_size, head_size)
    root_usable = jnp.ones((every_branch, root_keys.shape[0]), dtype=bool)
    root_part = partial_scores(grouped, root_keys, root_values, root_usable, scaling)
    local_mids = mid_keys.shape[0]
    node_ids = lax.axis_index("node") * local_mids + jnp.arange(local_mids, dtype=jnp.int32)
    routing = branch_mid[:, 0]
    matching = routing[None, :] == node_ids[:, None]
    ranking = jnp.cumsum(matching.astype(jnp.int32), axis=1) - 1
    selected = matching[:, None, :] & (
        ranking[:, None, :] == jnp.arange(CAP, dtype=jnp.int32)[None, :, None]
    )
    picked = jnp.einsum(
        "ncb,bkgd->nckgd",
        selected.astype(jnp.bfloat16),
        grouped,
        preferred_element_type=jnp.float32,
    ).astype(jnp.bfloat16)
    slot_index = jnp.arange(mid_keys.shape[1])

    def node_partial(inputs):
        node_queries, node_keys, node_values, node_id = inputs
        usable = jnp.broadcast_to(
            slot_index[None, :] < mid_length[node_id], (CAP, slot_index.shape[0])
        )
        return partial_scores(node_queries, node_keys, node_values, usable, scaling)

    node_high, node_totals, node_weighted = lax.map(
        node_partial, (picked, mid_keys, mid_values, node_ids)
    )
    chosen = selected.astype(jnp.float32)
    covered = jnp.sum(chosen, axis=(0, 1))
    back_high = (
        jnp.einsum("ncb,nckg->bkg", chosen, node_high, precision=lax.Precision.HIGHEST)
        + ((1.0 - covered) * masked_score)[:, None, None]
    )
    back_totals = jnp.einsum("ncb,nckg->bkg", chosen, node_totals, precision=lax.Precision.HIGHEST)
    back_weighted = jnp.einsum(
        "ncb,nckgd->bkgd", chosen, node_weighted, precision=lax.Precision.HIGHEST
    )
    shared_part = combine_parts(root_part, (back_high, back_totals, back_weighted))
    peaks, totals, weighted = (
        lax.all_to_all(shared_part[0], "node", split_axis=0, concat_axis=0, tiled=True),
        lax.all_to_all(shared_part[1], "node", split_axis=0, concat_axis=0, tiled=True),
        lax.all_to_all(shared_part[2], "node", split_axis=0, concat_axis=0, tiled=True),
    )
    peaks = peaks.reshape(node_count, owned, local_groups, group_size)
    totals = totals.reshape(node_count, owned, local_groups, group_size)
    weighted = weighted.reshape(node_count, owned, local_groups, group_size, head_size)
    highest = jnp.max(peaks, axis=0)
    factor = jnp.exp(peaks - highest[None])
    merged = (
        highest,
        jnp.sum(totals * factor, axis=0),
        jnp.sum(weighted * factor[..., None], axis=0),
    )
    own_grouped = queries.reshape(owned, local_groups, group_size, head_size)
    leaf_scores = (
        jnp.einsum("bkgd,blkd->bkgl", own_grouped, leaf_keys, preferred_element_type=jnp.float32)
        * scaling
    )
    leaf_usable = (jnp.arange(leaf_keys.shape[1])[None, :] < leaf_length[:, None])[:, None, None, :]
    leaf_scores = jnp.where(leaf_usable, leaf_scores, masked_score)
    leaf_peak = jnp.max(leaf_scores, axis=-1)
    leaf_weights = jnp.where(leaf_usable, jnp.exp(leaf_scores - leaf_peak[..., None]), 0.0)
    leaf_weighted = jnp.einsum(
        "bkgl,blkd->bkgd",
        leaf_weights.astype(jnp.bfloat16),
        leaf_values,
        preferred_element_type=jnp.float32,
    )
    final_part = combine_parts(merged, (leaf_peak, jnp.sum(leaf_weights, axis=-1), leaf_weighted))
    attended = (
        (final_part[2] / final_part[1][..., None])
        .reshape(owned, local_heads * head_size)
        .astype(jnp.bfloat16)
    )
    projected = jnp.dot(
        lax.all_gather(attended, "node", axis=0, tiled=True),
        out_weight,
        preferred_element_type=jnp.float32,
    )
    projected = lax.psum(projected.astype(jnp.bfloat16), "mp").astype(jnp.float32)
    stream = residual.astype(jnp.float32) + projected
    squares = lax.psum(jnp.sum(stream * stream, axis=1), "node")
    normed = (stream * lax.rsqrt(squares[:, None] / D + norm_eps) * norm_gain[None, :]).astype(
        jnp.bfloat16
    )
    out_rows = every_branch // lax.axis_size("mp")
    gate, upward = (
        lax.psum(
            jnp.dot(normed, gate_weight, preferred_element_type=jnp.float32).astype(jnp.bfloat16),
            "node",
        ).astype(jnp.float32),
        lax.psum(
            jnp.dot(normed, up_weight, preferred_element_type=jnp.float32).astype(jnp.bfloat16),
            "node",
        ).astype(jnp.float32),
    )
    act = (jax.nn.silu(gate) * upward).astype(jnp.bfloat16)
    mlp_rows = lax.psum_scatter(
        jnp.dot(act, down_weight, preferred_element_type=jnp.float32).astype(jnp.bfloat16),
        "mp",
        scatter_dimension=0,
        tiled=True,
    ).astype(jnp.float32)
    stream_rows = lax.dynamic_slice_in_dim(stream, lax.axis_index("mp") * out_rows, out_rows, 0)
    return (stream_rows + mlp_rows).astype(jnp.bfloat16)


def solution(mesh):
    in_specs = (
        P("node", "mp", None),
        P("node", "mp", None),
        P("node", "mp", None),
        P("node", None, "mp", None),
        P("node", None, "mp", None),
        P("node", None, "mp", None),
        P("node", None, "mp", None),
        P(),
        P("node"),
        P(),
        P(None, "node"),
        P("node"),
        P("mp", "node"),
        P("node", "mp"),
        P("node", "mp"),
        P("mp", "node"),
    )
    out_specs = P("mp", "node")
    return jax.shard_map(
        on_device, mesh=mesh, in_specs=in_specs, out_specs=out_specs, check_vma=False
    )
```

profile of v0, /device:TPU:0, one launch (start us, length us, event | category | flops | bytes accessed | tf_op | source)
XLA Modules:
  0.0 297.3 jit_solution(1106771095615868161)
XLA Ops:
  6.5 1.3 dynamic_slice.18
  9.5 32.5 %all_gather.6 = bf16[32,16,128]{2,1,0:T(8,128)(2,1)S(1)} all-gather(bf16[4,16,128]{2,1,0:T(8,128)(2,1)} %param.16), channel_id=1, replica_groups=mesh['node'=8,'mp'=4] {'node'}, dimensions={0}, use_global_device_ids=true | all-gather | bytes 147456 | tf_op jit(solution)/shard_map/all_gather | solution.py:64
  42.2 1.4 fusion.79
  44.0 2.1 bitcast_reduce_fusion
  46.2 1.8 copy-done.1
  49.7 5.5 %all-to-all-start.2 = ((f32[32,2,8]{2,1,0:T(2,128)}), f32[32,2,8]{2,1,0:T(2,128)S(1)}, u32[]{:S(2)}, u32[]{:S(2)}) async-start(f32[32,2,8]{2,1,0:T(2,128)} %copy.115), calls=%async_computation.2 | async-start | bytes 65536 | tf_op jit(solution)/shard_map/all_to_all | solution.py:108
  55.5 3.3 %fusion.13 = f32[32,2,8,128]{3,0,2,1:T(8,128)S(1)} fusion(f32[2,2048,32,8]{1,2,3,0:T(8,128)} %copy-done.1, f32[32,2,8]{0,2,1:T(8,128)S(1)} %get-tuple-element.48, bf16[2048,2,128,1]{2,1,0,3:T(2,128)(2,1)S(1)} %bitcast.75, f32[32,2,8]{0,2,1:T(8,128)S(1)} %subtract_exponential_fusion.2), kind=kOutput, calls=%fused_computation.16 | convolution fusion | flops 271646720 | bytes 5509120 | tf_op jit(solution)/shard_map/bkgl,lkd->bkgd/dot_general | solution.py:21
  59.9 2.0 all-to-all-done.2
  61.8 4.2 %all-to-all-start.1 = ((f32[32,2,8]{2,1,0:T(2,128)}), f32[32,2,8]{2,1,0:T(2,128)S(1)}, u32[]{:S(2)}, u32[]{:S(2)}) async-start(f32[32,2,8]{2,1,0:T(2,128)} %copy.104), calls=%async_computation.1 | async-start | bytes 65536 | tf_op jit(solution)/shard_map/all_to_all | solution.py:107
  66.3 0.8 copy.103
  67.2 5.5 %all-to-all-done.1 = f32[32,2,8]{2,1,0:T(2,128)S(1)} async-done(((f32[32,2,8]{2,1,0:T(2,128)}), f32[32,2,8]{2,1,0:T(2,128)S(1)}, u32[]{:S(2)}, u32[]{:S(2)}) %all-to-all-start.1) | async-done | bytes 2080 | tf_op jit(solution)/shard_map/all_to_all | solution.py:107
  72.7 3.4 %all-to-all-start = ((f32[32,2,8,128]{3,2,1,0:T(8,128)}), f32[32,2,8,128]{3,2,1,0:T(8,128)S(1)}, u32[]{:S(2)}, u32[]{:S(2)}) async-start(f32[32,2,8,128]{3,2,1,0:T(8,128)} %copy.103), calls=%async_computation | async-start | bytes 524288 | tf_op jit(solution)/shard_map/all_to_all | solution.py:109
  76.5 7.9 %all-to-all-done = f32[32,2,8,128]{3,2,1,0:T(8,128)S(1)} async-done(((f32[32,2,8,128]{3,2,1,0:T(8,128)}), f32[32,2,8,128]{3,2,1,0:T(8,128)S(1)}, u32[]{:S(2)}, u32[]{:S(2)}) %all-to-all-start) | async-done | bytes 262176 | tf_op jit(solution)/shard_map/all_to_all | solution.py:109
  84.8 30.6 %all-gather = bf16[8,4,2048]{2,1,0:T(4,128)(2,1)S(1)} all-gather(bf16[1,4,2048]{2,1,0:T(4,128)(2,1)S(1)} %reshape.273), channel_id=1, replica_groups=mesh['node'=8,'mp'=4] {'node'}, dimensions={0}, use_global_device_ids=true | all-gather | bytes 147456 | tf_op jit(solution)/shard_map/all_gather | solution.py:143
  115.4 3.6 %convolution_convert_fusion.3 = bf16[32,1024]{1,0:T(8,128)(2,1)} fusion(bf16[32,2048]{1,0:T(8,128)(2,1)S(1)} %reshape.274, bf16[2048,1024]{1,0:T(8,128)(2,1)} %param.28), kind=kOutput, calls=%fused_computation.20 | convolution fusion | flops 134250496 | bytes 4390912 | tf_op jit(solution)/shard_map/dot_general | solution.py:142
  119.1 30.0 %all-reduce.4.cloned.1.call-done = bf16[32,1024]{1,0:T(8,128)(2,1)} async-done(((bf16[32,1024]{1,0:T(8,128)(2,1)}), bf16[32,1024]{1,0:T(8,128)(2,1)}) %all-reduce.4.cloned.1.call-update) | async-done | bytes 65552 | tf_op jit(solution)/shard_map/psum | solution.py:147
  149.1 1.0 convert_add_fusion
  150.1 21.4 %psum.29 = f32[32]{0:T(128)S(1)} all-reduce(f32[32]{0:T(128)S(1)} %get-tuple-element.45), channel_id=1, replica_groups=mesh['node'=8,'mp'=4] {'node'}, use_global_device_ids=true, to_apply=%region_13.14 | all-reduce | flops 32 | bytes 256 | tf_op jit(solution)/shard_map/psum | solution.py:149
  171.4 8.7 %convolution_convert_fusion = bf16[32,7168]{1,0:T(8,128)(2,1)} fusion(bf16[1024,7168]{1,0:T(8,128)(2,1)} %param.30, f32[1024]{0:T(1024)S(1)} %copy-done.5, f32[32]{0:T(128)S(1)} %add_rsqrt_fusion, bf16[32,1024]{1,0:T(8,128)(2,1)} %all-reduce.4.cloned.1.call-done, bf16[32,1024]{1,0:T(8,128)(2,1)S(1)} %copy-done.2), kind=kOutput, calls=%fused_computation | convolution fusion | flops 470188032 | bytes 15274112 | tf_op jit(solution)/shard_map/dot_general | solution.py:160
  180.1 8.6 %convolution_convert_fusion.1 = bf16[32,7168]{1,0:T(8,128)(2,1)} fusion(bf16[1024,7168]{1,0:T(8,128)(2,1)} %param.29, f32[1024]{0:T(1024)S(1)} %copy-done.5, f32[32]{0:T(128)S(1)} %add_rsqrt_fusion, bf16[32,1024]{1,0:T(8,128)(2,1)S(1)} %copy-done.3, bf16[32,1024]{1,0:T(8,128)(2,1)S(1)} %copy-done.2), kind=kOutput, calls=%fused_computation.1 | convolution fusion | flops 470188032 | bytes 15274112 | tf_op jit(solution)/shard_map/dot_general | solution.py:156
  188.8 73.1 %all-reduce.6.cloned.1.call-done = (bf16[32,7168]{1,0:T(8,128)(2,1)}, bf16[32,7168]{1,0:T(8,128)(2,1)}) async-done(((bf16[32,7168]{1,0:T(8,128)(2,1)}, bf16[32,7168]{1,0:T(8,128)(2,1)}), (bf16[32,7168]{1,0:T(8,128)(2,1)}, bf16[32,7168]{1,0:T(8,128)(2,1)})) %all-reduce.6.cloned.1.call-update) | async-done | bytes 917520 | tf_op jit(solution)/shard_map/psum | solution.py:159
  261.8 8.7 %convolution_convert_fusion.2 = bf16[32,1024]{1,0:T(8,128)(2,1)} fusion(bf16[7168,1024]{1,0:T(8,128)(2,1)} %param.31, bf16[32,7168]{1,0:T(8,128)(2,1)} %get-tuple-element.23, bf16[32,7168]{1,0:T(8,128)(2,1)} %get-tuple-element.24), kind=kOutput, calls=%fused_computation.19 | convolution fusion | flops 471629824 | bytes 15663104 | tf_op jit(solution)/shard_map/dot_general | solution.py:166
  270.6 18.8 %reduce-scatter.2.cloned.1.call-done = bf16[8,1024]{1,0:T(8,128)(2,1)} async-done(((bf16[32,1024]{1,0:T(8,128)(2,1)}), bf16[8,1024]{1,0:T(8,128)(2,1)}) %reduce-scatter.2.cloned.1.call-update) | async-done | bytes 16400 | tf_op jit(solution)/shard_map/reduce_scatter | solution.py:165
  289.4 1.3 add_convert_fusion
  (61 shorter events, 6.5 us)
Async XLA Ops:
  6.5 49.0 %copy-start = (bf16[2048,2,128]{2,1,0:T(2,128)(2,1)S(1)}, bf16[2048,2,128]{2,1,0:T(2,128)(2,1)}, u32[]{:S(2)}) copy-start(bf16[2048,2,128]{2,1,0:T(2,128)(2,1)} %param.18) | copy-start | bytes 3145732
  44.0 11.1 %copy-start.9 = (s32[4]{0:T(128)S(1)}, s32[4]{0:T(128)}, u32[]{:S(2)}) copy-start(s32[4]{0:T(128)} %param.24) | copy-start | bytes 52
  44.0 11.2 %copy-start.7 = (bf16[1,1024,2,128]{3,2,1,0:T(2,128)(2,1)S(1)}, bf16[1,1024,2,128]{3,2,1,0:T(2,128)(2,1)}, u32[]{:S(2)}) copy-start(bf16[1,1024,2,128]{3,2,1,0:T(2,128)(2,1)} %param.20) | copy-start | bytes 1572868
  46.1 1.9 copy-start.1
  48.9 10.0 %copy-start.4 = (bf16[4,256,2,128]{3,2,1,0:T(2,128)(2,1)S(1)}, bf16[4,256,2,128]{3,2,1,0:T(2,128)(2,1)}, u32[]{:S(2)}) copy-start(bf16[4,256,2,128]{3,2,1,0:T(2,128)(2,1)} %param.21) | copy-start | bytes 1572868
  48.9 10.0 %copy-start.6 = (bf16[4,16,128]{2,1,0:T(8,128)(2,1)S(1)}, bf16[4,16,128]{2,1,0:T(8,128)(2,1)}, u32[]{:S(2)}) copy-start(bf16[4,16,128]{2,1,0:T(8,128)(2,1)} %param.16) | copy-start | bytes 49156
  49.7 12.1 %all-to-all-start.2 = ((f32[32,2,8]{2,1,0:T(2,128)}), f32[32,2,8]{2,1,0:T(2,128)S(1)}, u32[]{:S(2)}, u32[]{:S(2)}) async-start(f32[32,2,8]{2,1,0:T(2,128)} %copy.115), calls=%async_computation.2 | async-start | bytes 65536 | tf_op jit(solution)/shard_map/all_to_all | solution.py:108
  55.5 29.0 %copy-start.8 = (bf16[4,256,2,128]{3,2,1,0:T(2,128)(2,1)S(1)}, bf16[4,256,2,128]{3,2,1,0:T(2,128)(2,1)}, u32[]{:S(2)}) copy-start(bf16[4,256,2,128]{3,2,1,0:T(2,128)(2,1)} %param.22) | copy-start | bytes 1572868
  59.9 89.2 %copy-start.2 = (bf16[32,1024]{1,0:T(8,128)(2,1)S(1)}, bf16[32,1024]{1,0:T(8,128)(2,1)}, u32[]{:S(2)}) copy-start(bf16[32,1024]{1,0:T(8,128)(2,1)} %param.26) | copy-start | bytes 196612
  61.8 10.9 %all-to-all-start.1 = ((f32[32,2,8]{2,1,0:T(2,128)}), f32[32,2,8]{2,1,0:T(2,128)S(1)}, u32[]{:S(2)}, u32[]{:S(2)}) async-start(f32[32,2,8]{2,1,0:T(2,128)} %copy.104), calls=%async_computation.1 | async-start | bytes 65536 | tf_op jit(solution)/shard_map/all_to_all | solution.py:107
  66.0 105.4 %copy-start.5 = (f32[1024]{0:T(1024)S(1)}, f32[1024]{0:T(1024)}, u32[]{:S(2)}) copy-start(f32[1024]{0:T(1024)} %param.27) | copy-start | bytes 12292
  72.7 11.7 %all-to-all-start = ((f32[32,2,8,128]{3,2,1,0:T(8,128)}), f32[32,2,8,128]{3,2,1,0:T(8,128)S(1)}, u32[]{:S(2)}, u32[]{:S(2)}) async-start(f32[32,2,8,128]{3,2,1,0:T(8,128)} %copy.103), calls=%async_computation | async-start | bytes 524288 | tf_op jit(solution)/shard_map/all_to_all | solution.py:109
  76.1 73.0 %all-reduce.4.cloned.1.call-start = ((), (), s32[]{:S(2)}) async-start(), calls=%async_computation.4 | async-start | bytes 131072 | tf_op jit(solution)/shard_map/psum | solution.py:147
  119.0 142.8 %all-reduce.6.cloned.1.call-start = ((), (), s32[]{:S(2)}) async-start(), calls=%async_computation.6 | async-start | bytes 1835008 | tf_op jit(solution)/shard_map/psum | solution.py:159
  171.4 8.7 %copy-start.3 = (bf16[32,1024]{1,0:T(8,128)(2,1)S(1)}, bf16[32,1024]{1,0:T(8,128)(2,1)}, u32[]{:S(2)}) copy-start(bf16[32,1024]{1,0:T(8,128)(2,1)} %all-reduce.4.cloned.1.call-done) | copy-start | bytes 196612
  188.7 100.7 %reduce-scatter.2.cloned.1.call-start = ((), (), s32[]{:S(2)}) async-start(), calls=%async_computation.5 | async-start | bytes 81920 | tf_op jit(solution)/shard_map/reduce_scatter | solution.py:165
Sparse Core Ops, SparseCore 0:
  119.1 29.9 all-reduce.3
  188.9 72.9 all-reduce.5
  270.7 18.6 reduce-scatter.1
where the time goes:
time: 298 us; the launch traced here: 297 us
  waiting for transfers between devices  137 us (46%)
  blocking collectives  84.5 us (28%)
  matrix products  38 us (13%)
  between operations  13.3 us (4%)
  starting transfers between devices  13.1 us (4%)
  local copies, waits for them, and re-layouts  5.71 us (2%)
  other arithmetic  5.33 us (2%)
    psum x1, waiting for transfers between devices, on_device(): lax.psum(jnp.dot(normed, up_weight, preferred_element_type=jnp.float32).a...  73.1 us
    all_gather x1, blocking collectives, on_device(): gathered = lax.all_gather(queries, 'node', axis=0, tiled=True)  32.5 us
    all_gather x1, blocking collectives, on_device(): lax.all_gather(attended, 'node', axis=0, tiled=True)  30.6 us
    psum x1, waiting for transfers between devices, on_device(): lax.psum(projected.astype(jnp.bfloat16), 'mp').astype(jnp.float32)  30 us
    psum x1, blocking collectives, on_device(): squares = lax.psum(jnp.sum(stream * stream, axis=1), 'node')  21.4 us
    reduce_scatter x1, waiting for transfers between devices, on_device(): lax.psum_scatter(jnp.dot(act, down_weight, preferred_element_type=jnp.flo...  18.8 us
    dot_general x1, matrix products, on_device(): jnp.dot(act, down_weight, preferred_element_type=jnp.float32)  8.71 us
    dot_general x1, matrix products, on_device(): jnp.dot(normed, up_weight, preferred_element_type=jnp.float32)  8.67 us
  transfers between devices with their start and end apart: 6, of which 6 were waited for; matrix products, arithmetic and copies ran while one was open for 2% of the time, Pallas kernels for 0%

commit v1 on v0

--- a/solution.py
+++ b/solution.py
@@ -61,7 +61,12 @@
     group_size = local_heads // local_groups
     scaling = head_size ** (-0.5)
     node_count = lax.axis_size("node")
-    gathered = lax.all_gather(queries, "node", axis=0, tiled=True)
+    ring = [queries]
+    for hop in range(7):
+        ring.append(lax.ppermute(ring[-1], "node", [(dev, (dev + 1) % 8) for dev in range(8)]))
+    gathered = jnp.roll(
+        jnp.concatenate(ring[::-1], axis=0), (lax.axis_index("node") + 1) * ring[0].shape[0], axis=0
+    )
     every_branch = gathered.shape[0]
     grouped = gathered.reshape(every_branch, local_groups, group_size, head_size)
     root_usable = jnp.ones((every_branch, root_keys.shape[0]), dtype=bool)

time: 298 us -> 308 us (1.034)
  waiting for transfers between devices: 137 us -> 174 us
  blocking collectives: 84.5 us -> 51.9 us
    ppermute x0 -> x7, waiting for transfers between devices: none -> 38.6 us  [on_device(): lax.ppermute(ring[-1], 'node', [(dev, (dev + 1) % 8) for dev in range(8)])]
    all_gather x1 -> x0, blocking collectives: 32.5 us -> none  [on_device(): gathered = lax.all_gather(queries, 'node', axis=0, tiled=True)]
  transfers between devices with their start and end apart: 6 -> 13, of which waited for: 6 -> 13; matrix products, arithmetic and copies ran while one was open for 2% -> 4% of each run, Pallas kernels for 0% -> 0%
where the time goes in v1:
time: 308 us; the launch traced here: 307 us
  waiting for transfers between devices  174 us (56%)
  blocking collectives  51.9 us (17%)
  matrix products  40.4 us (13%)
  between operations  13.4 us (4%)
  starting transfers between devices  13.2 us (4%)
  other arithmetic  8.14 us (3%)
  local copies, waits for them, and re-layouts  5.56 us (2%)
    psum x1, waiting for transfers between devices, on_device(): lax.psum(jnp.dot(normed, up_weight, preferred_element_type=jnp.float32).a...  73.2 us
    ppermute x7, waiting for transfers between devices, on_device(): lax.ppermute(ring[-1], 'node', [(dev, (dev + 1) % 8) for dev in range(8)])  38.6 us
    all_gather x1, blocking collectives, on_device(): lax.all_gather(attended, 'node', axis=0, tiled=True)  30.5 us
    psum x1, waiting for transfers between devices, on_device(): lax.psum(projected.astype(jnp.bfloat16), 'mp').astype(jnp.float32)  30.2 us
    psum x1, blocking collectives, on_device(): squares = lax.psum(jnp.sum(stream * stream, axis=1), 'node')  21.4 us
    reduce_scatter x1, waiting for transfers between devices, on_device(): lax.psum_scatter(jnp.dot(act, down_weight, preferred_element_type=jnp.flo...  18.8 us
    dot_general x1, matrix products, on_device(): jnp.dot(act, down_weight, preferred_element_type=jnp.float32)  8.71 us
    dot_general x1, matrix products, on_device(): jnp.dot(normed, up_weight, preferred_element_type=jnp.float32)  8.67 us
  transfers between devices with their start and end apart: 13, of which 13 were waited for; matrix products, arithmetic and copies ran while one was open for 4% of the time, Pallas kernels for 0%

profile of v1, /device:TPU:0, one launch (start us, length us, event | category | flops | bytes accessed | tf_op | source)
XLA Modules:
  0.0 306.9 jit_solution(13024679936554392162)
XLA Ops:
  6.5 3.0 collective-permute-start
  10.2 4.2 %collective-permute-done = bf16[4,16,128]{2,1,0:T(8,128)(2,1)S(1)} collective-permute-done((bf16[4,16,128]{2,1,0:T(8,128)(2,1)}, bf16[4,16,128]{2,1,0:T(8,128)(2,1)S(1)}, u32[]{:S(2)}, u32[]{:S(2)}) %collective-permute-start) | collective-permute-done | bytes 16416 | tf_op jit(solution)/shard_map/ppermute | solution.py:66
  15.9 5.0 %collective-permute-done.1 = bf16[4,16,128]{2,1,0:T(8,128)(2,1)S(1)} collective-permute-done((bf16[4,16,128]{2,1,0:T(8,128)(2,1)S(1)}, bf16[4,16,128]{2,1,0:T(8,128)(2,1)S(1)}, u32[]{:S(2)}, u32[]{:S(2)}) %collective-permute-start.1) | collective-permute-done | bytes 16416 | tf_op jit(solution)/shard_map/ppermute | solution.py:66
  21.7 5.6 %collective-permute-done.2 = bf16[4,16,128]{2,1,0:T(8,128)(2,1)S(1)} collective-permute-done((bf16[4,16,128]{2,1,0:T(8,128)(2,1)S(1)}, bf16[4,16,128]{2,1,0:T(8,128)(2,1)S(1)}, u32[]{:S(2)}, u32[]{:S(2)}) %collective-permute-start.2) | collective-permute-done | bytes 16416 | tf_op jit(solution)/shard_map/ppermute | solution.py:66
  27.5 6.3 %collective-permute-done.3 = bf16[4,16,128]{2,1,0:T(8,128)(2,1)S(1)} collective-permute-done((bf16[4,16,128]{2,1,0:T(8,128)(2,1)S(1)}, bf16[4,16,128]{2,1,0:T(8,128)(2,1)S(1)}, u32[]{:S(2)}, u32[]{:S(2)}) %collective-permute-start.3) | collective-permute-done | bytes 16416 | tf_op jit(solution)/shard_map/ppermute | solution.py:66
  33.8 6.4 %collective-permute-done.4 = bf16[4,16,128]{2,1,0:T(8,128)(2,1)S(1)} collective-permute-done((bf16[4,16,128]{2,1,0:T(8,128)(2,1)S(1)}, bf16[4,16,128]{2,1,0:T(8,128)(2,1)S(1)}, u32[]{:S(2)}, u32[]{:S(2)}) %collective-permute-start.4) | collective-permute-done | bytes 16416 | tf_op jit(solution)/shard_map/ppermute | solution.py:66
  41.5 5.2 %collective-permute-done.5 = bf16[4,16,128]{2,1,0:T(8,128)(2,1)S(1)} collective-permute-done((bf16[4,16,128]{2,1,0:T(8,128)(2,1)S(1)}, bf16[4,16,128]{2,1,0:T(8,128)(2,1)S(1)}, u32[]{:S(2)}, u32[]{:S(2)}) %collective-permute-start.5) | collective-permute-done | bytes 16416 | tf_op jit(solution)/shard_map/ppermute | solution.py:66
  47.3 5.8 %collective-permute-done.6 = bf16[4,16,128]{2,1,0:T(8,128)(2,1)S(1)} collective-permute-done((bf16[4,16,128]{2,1,0:T(8,128)(2,1)S(1)}, bf16[4,16,128]{2,1,0:T(8,128)(2,1)S(1)}, u32[]{:S(2)}, u32[]{:S(2)}) %collective-permute-start.6) | collective-permute-done | bytes 16416 | tf_op jit(solution)/shard_map/ppermute | solution.py:66
  61.9 3.3 %all-to-all-start.1 = ((f32[32,2,8]{2,1,0:T(2,128)}), f32[32,2,8]{2,1,0:T(2,128)S(1)}, u32[]{:S(2)}, u32[]{:S(2)}) async-start(f32[32,2,8]{2,1,0:T(2,128)} %copy.123), calls=%async_computation.1 | async-start | bytes 65536 | tf_op jit(solution)/shard_map/all_to_all | solution.py:112
  65.2 3.0 fusion.1
  71.9 3.4 %all-to-all-start.2 = ((f32[32,2,8]{2,1,0:T(2,128)}), f32[32,2,8]{2,1,0:T(2,128)S(1)}, u32[]{:S(2)}, u32[]{:S(2)}) async-start(f32[32,2,8]{2,1,0:T(2,128)} %copy.135), calls=%async_computation.2 | async-start | bytes 65536 | tf_op jit(solution)/shard_map/all_to_all | solution.py:113
  75.2 3.1 %fusion.15 = f32[32,2,8,128]{3,2,0,1:T(8,128)S(1)} fusion(f32[2,32,8,2048]{3,2,1,0:T(8,128)} %get-tuple-element.49, f32[32,2,8]{2,0,1:T(8,128)S(1)} %get-tuple-element.48, bf16[2048,2,128,1]{2,1,0,3:T(2,128)(2,1)S(1)} %bitcast.84, f32[32,2,8,128]{3,0,2,1:T(8,128)S(1)} %fusion.48, f32[32,2,8]{2,0,1:T(8,128)S(1)} %copy.120, f32[32,2,8]{2,0,1:T(8,128)S(1)} %copy.117), kind=kOutput, calls=%fused_computation.15 | convolution fusion | flops 271777792 | bytes 5773312 | tf_op jit(solution)/shard_map/bkgl,lkd->bkgd/dot_general | solution.py:21
  79.1 3.0 all-to-all-done.2
  82.0 3.4 %all-to-all-start = ((f32[32,2,8,128]{3,2,1,0:T(8,128)}), f32[32,2,8,128]{3,2,1,0:T(8,128)S(1)}, u32[]{:S(2)}, u32[]{:S(2)}) async-start(f32[32,2,8,128]{3,2,1,0:T(8,128)} %copy.122), calls=%async_computation | async-start | bytes 524288 | tf_op jit(solution)/shard_map/all_to_all | solution.py:114
  85.8 7.9 %all-to-all-done = f32[32,2,8,128]{3,2,1,0:T(8,128)S(1)} async-done(((f32[32,2,8,128]{3,2,1,0:T(8,128)}), f32[32,2,8,128]{3,2,1,0:T(8,128)S(1)}, u32[]{:S(2)}, u32[]{:S(2)}) %all-to-all-start) | async-done | bytes 262176 | tf_op jit(solution)/shard_map/all_to_all | solution.py:114
  94.1 30.5 %all-gather = bf16[8,4,2048]{2,1,0:T(4,128)(2,1)S(1)} all-gather(bf16[1,4,2048]{2,1,0:T(4,128)(2,1)S(1)} %reshape.273), channel_id=1, replica_groups=mesh['node'=8,'mp'=4] {'node'}, dimensions={0}, use_global_device_ids=true | all-gather | bytes 147456 | tf_op jit(solution)/shard_map/all_gather | solution.py:148
  124.7 3.6 %convolution_convert_fusion.3 = bf16[32,1024]{1,0:T(8,128)(2,1)} fusion(bf16[32,2048]{1,0:T(8,128)(2,1)S(1)} %reshape.274, bf16[2048,1024]{1,0:T(8,128)(2,1)} %param.28), kind=kOutput, calls=%fused_computation.19 | convolution fusion | flops 134250496 | bytes 4390912 | tf_op jit(solution)/shard_map/dot_general | solution.py:147
  128.4 30.2 %all-reduce.4.cloned.1.call-done = bf16[32,1024]{1,0:T(8,128)(2,1)} async-done(((bf16[32,1024]{1,0:T(8,128)(2,1)}), bf16[32,1024]{1,0:T(8,128)(2,1)}) %all-reduce.4.cloned.1.call-update) | async-done | bytes 65552 | tf_op jit(solution)/shard_map/psum | solution.py:152
  159.6 21.4 %psum.29 = f32[32]{0:T(128)S(1)} all-reduce(f32[32]{0:T(128)S(1)} %get-tuple-element.45), channel_id=1, replica_groups=mesh['node'=8,'mp'=4] {'node'}, use_global_device_ids=true, to_apply=%region_13.14 | all-reduce | flops 32 | bytes 256 | tf_op jit(solution)/shard_map/psum | solution.py:154
  181.0 8.7 %convolution_convert_fusion = bf16[32,7168]{1,0:T(8,128)(2,1)} fusion(bf16[1024,7168]{1,0:T(8,128)(2,1)} %param.30, f32[1024]{0:T(1024)S(1)} %copy-done.3, f32[32]{0:T(128)S(1)} %add_rsqrt_fusion, bf16[32,1024]{1,0:T(8,128)(2,1)} %all-reduce.4.cloned.1.call-done, bf16[32,1024]{1,0:T(8,128)(2,1)S(1)} %copy-done.1), kind=kOutput, calls=%fused_computation | convolution fusion | flops 470188032 | bytes 15274112 | tf_op jit(solution)/shard_map/dot_general | solution.py:165
  189.6 8.6 %convolution_convert_fusion.1 = bf16[32,7168]{1,0:T(8,128)(2,1)} fusion(bf16[1024,7168]{1,0:T(8,128)(2,1)} %param.29, f32[1024]{0:T(1024)S(1)} %copy-done.3, f32[32]{0:T(128)S(1)} %add_rsqrt_fusion, bf16[32,1024]{1,0:T(8,128)(2,1)S(1)} %copy-done.2, bf16[32,1024]{1,0:T(8,128)(2,1)S(1)} %copy-done.1), kind=kOutput, calls=%fused_computation.1 | convolution fusion | flops 470188032 | bytes 15274112 | tf_op jit(solution)/shard_map/dot_general | solution.py:161
  198.3 73.2 %all-reduce.6.cloned.1.call-done = (bf16[32,7168]{1,0:T(8,128)(2,1)}, bf16[32,7168]{1,0:T(8,128)(2,1)}) async-done(((bf16[32,7168]{1,0:T(8,128)(2,1)}, bf16[32,7168]{1,0:T(8,128)(2,1)}), (bf16[32,7168]{1,0:T(8,128)(2,1)}, bf16[32,7168]{1,0:T(8,128)(2,1)})) %all-reduce.6.cloned.1.call-update) | async-done | bytes 917520 | tf_op jit(solution)/shard_map/psum | solution.py:164
  271.5 8.7 %convolution_convert_fusion.2 = bf16[32,1024]{1,0:T(8,128)(2,1)} fusion(bf16[7168,1024]{1,0:T(8,128)(2,1)} %param.31, bf16[32,7168]{1,0:T(8,128)(2,1)} %get-tuple-element.23, bf16[32,7168]{1,0:T(8,128)(2,1)} %get-tuple-element.24), kind=kOutput, calls=%fused_computation.18 | convolution fusion | flops 471629824 | bytes 15663104 | tf_op jit(solution)/shard_map/dot_general | solution.py:171
  280.2 18.8 %reduce-scatter.2.cloned.1.call-done = bf16[8,1024]{1,0:T(8,128)(2,1)} async-done(((bf16[32,1024]{1,0:T(8,128)(2,1)}), bf16[8,1024]{1,0:T(8,128)(2,1)}) %reduce-scatter.2.cloned.1.call-update) | async-done | bytes 16400 | tf_op jit(solution)/shard_map/reduce_scatter | solution.py:170
  (86 shorter events, 21.2 us)
Async XLA Ops:
  6.5 51.8 %copy-start = (bf16[2048,2,128]{2,1,0:T(2,128)(2,1)S(1)}, bf16[2048,2,128]{2,1,0:T(2,128)(2,1)}, u32[]{:S(2)}) copy-start(bf16[2048,2,128]{2,1,0:T(2,128)(2,1)} %param.17) | copy-start | bytes 3145732
  6.5 7.9 %collective-permute-start = (bf16[4,16,128]{2,1,0:T(8,128)(2,1)}, bf16[4,16,128]{2,1,0:T(8,128)(2,1)S(1)}, u32[]{:S(2)}, u32[]{:S(2)}) collective-permute-start(bf16[4,16,128]{2,1,0:T(8,128)(2,1)} %param.16), channel_id=1, source_target_pairs={{0,4},{4,8},{8,12},{12,16},{16,20},{20,24},{24,28},{28,0},{1,5},{5... | collective-permute-start | bytes 49160 | tf_op jit(solution)/shard_map/ppermute | solution.py:66
  14.5 6.4 %collective-permute-start.1 = (bf16[4,16,128]{2,1,0:T(8,128)(2,1)S(1)}, bf16[4,16,128]{2,1,0:T(8,128)(2,1)S(1)}, u32[]{:S(2)}, u32[]{:S(2)}) collective-permute-start(bf16[4,16,128]{2,1,0:T(8,128)(2,1)S(1)} %collective-permute-done), channel_id=1, source_target_pairs={{0,4},{4,8},{8,12},{12,16},{16,20},{20,24},{24,28},{28,0},{1,5},{5... | collective-permute-start | bytes 49160 | tf_op jit(solution)/shard_map/ppermute | solution.py:66
  20.9 6.4 %collective-permute-start.2 = (bf16[4,16,128]{2,1,0:T(8,128)(2,1)S(1)}, bf16[4,16,128]{2,1,0:T(8,128)(2,1)S(1)}, u32[]{:S(2)}, u32[]{:S(2)}) collective-permute-start(bf16[4,16,128]{2,1,0:T(8,128)(2,1)S(1)} %collective-permute-done.1), channel_id=1, source_target_pairs={{0,4},{4,8},{8,12},{12,16},{16,20},{20,24},{24,28},{28,0},{1,5},{5... | collective-permute-start | bytes 49160 | tf_op jit(solution)/shard_map/ppermute | solution.py:66
  27.3 6.4 %collective-permute-start.3 = (bf16[4,16,128]{2,1,0:T(8,128)(2,1)S(1)}, bf16[4,16,128]{2,1,0:T(8,128)(2,1)S(1)}, u32[]{:S(2)}, u32[]{:S(2)}) collective-permute-start(bf16[4,16,128]{2,1,0:T(8,128)(2,1)S(1)} %collective-permute-done.2), channel_id=1, source_target_pairs={{0,4},{4,8},{8,12},{12,16},{16,20},{20,24},{24,28},{28,0},{1,5},{5... | collective-permute-start | bytes 49160 | tf_op jit(solution)/shard_map/ppermute | solution.py:66
  33.8 6.4 %collective-permute-start.4 = (bf16[4,16,128]{2,1,0:T(8,128)(2,1)S(1)}, bf16[4,16,128]{2,1,0:T(8,128)(2,1)S(1)}, u32[]{:S(2)}, u32[]{:S(2)}) collective-permute-start(bf16[4,16,128]{2,1,0:T(8,128)(2,1)S(1)} %collective-permute-done.3), channel_id=1, source_target_pairs={{0,4},{4,8},{8,12},{12,16},{16,20},{20,24},{24,28},{28,0},{1,5},{5... | collective-permute-start | bytes 49160 | tf_op jit(solution)/shard_map/ppermute | solution.py:66
  40.2 6.4 %collective-permute-start.5 = (bf16[4,16,128]{2,1,0:T(8,128)(2,1)S(1)}, bf16[4,16,128]{2,1,0:T(8,128)(2,1)S(1)}, u32[]{:S(2)}, u32[]{:S(2)}) collective-permute-start(bf16[4,16,128]{2,1,0:T(8,128)(2,1)S(1)} %collective-permute-done.4), channel_id=1, source_target_pairs={{0,4},{4,8},{8,12},{12,16},{16,20},{20,24},{24,28},{28,0},{1,5},{5... | collective-permute-start | bytes 49160 | tf_op jit(solution)/shard_map/ppermute | solution.py:66
  46.7 6.4 %collective-permute-start.6 = (bf16[4,16,128]{2,1,0:T(8,128)(2,1)S(1)}, bf16[4,16,128]{2,1,0:T(8,128)(2,1)S(1)}, u32[]{:S(2)}, u32[]{:S(2)}) collective-permute-start(bf16[4,16,128]{2,1,0:T(8,128)(2,1)S(1)} %collective-permute-done.5), channel_id=1, source_target_pairs={{0,4},{4,8},{8,12},{12,16},{16,20},{20,24},{24,28},{28,0},{1,5},{5... | collective-permute-start | bytes 49160 | tf_op jit(solution)/shard_map/ppermute | solution.py:66
  58.3 16.9 %copy-start.4 = (bf16[2048,2,128]{2,1,0:T(2,128)(2,1)S(1)}, bf16[2048,2,128]{2,1,0:T(2,128)(2,1)}, u32[]{:S(2)}) copy-start(bf16[2048,2,128]{2,1,0:T(2,128)(2,1)} %param.18) | copy-start | bytes 3145732
  61.9 10.0 %all-to-all-start.1 = ((f32[32,2,8]{2,1,0:T(2,128)}), f32[32,2,8]{2,1,0:T(2,128)S(1)}, u32[]{:S(2)}, u32[]{:S(2)}) async-start(f32[32,2,8]{2,1,0:T(2,128)} %copy.123), calls=%async_computation.1 | async-start | bytes 65536 | tf_op jit(solution)/shard_map/all_to_all | solution.py:112
  68.2 25.6 %copy-start.5 = (bf16[4,256,2,128]{3,2,1,0:T(2,128)(2,1)S(1)}, bf16[4,256,2,128]{3,2,1,0:T(2,128)(2,1)}, u32[]{:S(2)}) copy-start(bf16[4,256,2,128]{3,2,1,0:T(2,128)(2,1)} %param.22) | copy-start | bytes 1572868
  71.9 10.2 %all-to-all-start.2 = ((f32[32,2,8]{2,1,0:T(2,128)}), f32[32,2,8]{2,1,0:T(2,128)S(1)}, u32[]{:S(2)}, u32[]{:S(2)}) async-start(f32[32,2,8]{2,1,0:T(2,128)} %copy.135), calls=%async_computation.2 | async-start | bytes 65536 | tf_op jit(solution)/shard_map/all_to_all | solution.py:113
  78.3 80.3 %copy-start.1 = (bf16[32,1024]{1,0:T(8,128)(2,1)S(1)}, bf16[32,1024]{1,0:T(8,128)(2,1)}, u32[]{:S(2)}) copy-start(bf16[32,1024]{1,0:T(8,128)(2,1)} %param.26) | copy-start | bytes 196612
  78.3 102.6 %copy-start.3 = (f32[1024]{0:T(1024)S(1)}, f32[1024]{0:T(1024)}, u32[]{:S(2)}) copy-start(f32[1024]{0:T(1024)} %param.27) | copy-start | bytes 12292
  82.0 11.7 %all-to-all-start = ((f32[32,2,8,128]{3,2,1,0:T(8,128)}), f32[32,2,8,128]{3,2,1,0:T(8,128)S(1)}, u32[]{:S(2)}, u32[]{:S(2)}) async-start(f32[32,2,8,128]{3,2,1,0:T(8,128)} %copy.122), calls=%async_computation | async-start | bytes 524288 | tf_op jit(solution)/shard_map/all_to_all | solution.py:114
  85.5 73.2 %all-reduce.4.cloned.1.call-start = ((), (), s32[]{:S(2)}) async-start(), calls=%async_computation.4 | async-start | bytes 131072 | tf_op jit(solution)/shard_map/psum | solution.py:152
  128.4 143.2 %all-reduce.6.cloned.1.call-start = ((), (), s32[]{:S(2)}) async-start(), calls=%async_computation.6 | async-start | bytes 1835008 | tf_op jit(solution)/shard_map/psum | solution.py:164
  181.0 8.7 %copy-start.2 = (bf16[32,1024]{1,0:T(8,128)(2,1)S(1)}, bf16[32,1024]{1,0:T(8,128)(2,1)}, u32[]{:S(2)}) copy-start(bf16[32,1024]{1,0:T(8,128)(2,1)} %all-reduce.4.cloned.1.call-done) | copy-start | bytes 196612
  198.3 100.8 %reduce-scatter.2.cloned.1.call-start = ((), (), s32[]{:S(2)}) async-start(), calls=%async_computation.5 | async-start | bytes 81920 | tf_op jit(solution)/shard_map/reduce_scatter | solution.py:170
Sparse Core Ops, SparseCore 0:
  128.5 30.1 all-reduce.3
  198.4 73.0 all-reduce.5
  280.4 18.6 reduce-scatter.1
